TPU v7x, 128 devices: a whole 4x4x4 slice. The times are simulated.
128 devices in a mesh: row: 16 (over x, z), col: 8 (over y, core).
Axes of the slice: x: 4, y: 4, z: 4, core: 2. Of those that a mesh axis runs over, the one named last changes fastest.
Arguments:
- primal_rows: bfloat16 [16384, 8192], P('row', 'col'), may hold values from -6 to 6
- dual_rows: bfloat16 [16384, 8192], P('row', 'col'), may hold values from -6 to 6
- weight_rows: bfloat16 [16384, 8192], P('row', 'col'), may hold values from -0.0625 to 0.0625
- pairs: int32 [384, 2], P('row'), may hold values from 0 to 63, as said below
Outputs:
- tiles: float32 [384, 256, 256], P('row', 'col')
Inputs may be any that keep to these rules, and one draw needn't show every extreme that they name: `pairs`: tile rows r * 24 to (r + 1) * 24 - 1 have their first block i among blocks r * 4 to (r + 1) * 4 - 1. Among their second blocks j, the blocks held by any other row index q (blocks q * 4 to (q + 1) * 4 - 1) are exactly one block, named one or more times; blocks of r itself may appear too.
All inputs are finite; a program needn't handle non-finite values.
Results may differ from a plain program's by a relative error of at most 0.0003.
Values may be sent and summed in bfloat16 or wider, within the bound.
No kernel may reach another device: no remote copies, remote signals or barrier semaphores. Data moves between devices by JAX's collectives and lax.ppermute only.
A program may use at most 128 MiB of HBM per device.

v0:
```python
import jax
import jax.numpy as jnp
from jax import lax
from jax.sharding import PartitionSpec as P

TILE = 256


def shards(primal_rows, dual_rows, weight_rows, pairs):
    row_count = lax.axis_size("row")
    my_row = lax.axis_index("row")
    per_row = primal_rows.shape[0] // TILE
    features = primal_rows.shape[1]
    tile_count = pairs.shape[0]
    every_pair = lax.all_gather(pairs, "row", axis=0, tiled=True)
    wanted = every_pair.reshape(row_count, tile_count * 2)
    held_here = wanted // per_row == my_row
    local_pick = jnp.max(jnp.where(held_here, wanted - my_row * per_row, 0), axis=1)
    weight_blocks = weight_rows.reshape(per_row, TILE, features)
    outgoing = jnp.take(weight_blocks, local_pick, axis=0)
    incoming = lax.all_to_all(outgoing, "row", split_axis=0, concat_axis=0, tiled=True)
    block_table = jnp.concatenate([weight_blocks, incoming], axis=0)
    first_local = pairs[:, 0] - my_row * per_row
    second_block = pairs[:, 1]
    second_row = second_block // per_row
    second_slot = jnp.where(
        second_row == my_row, second_block - my_row * per_row, per_row + second_row
    )
    left_x = jnp.take(primal_rows.reshape(per_row, TILE, features), first_local, axis=0)
    left_s = jnp.take(dual_rows.reshape(per_row, TILE, features), first_local, axis=0)
    right_rows = jnp.take(block_table, second_slot, axis=0)
    cross_x = jnp.einsum("tak,tbk->tab", left_x, right_rows, preferred_element_type=jnp.float32)
    cross_s = jnp.einsum("tak,tbk->tab", left_s, right_rows, preferred_element_type=jnp.float32)
    stacked = jnp.stack([cross_x, cross_s])
    whole = lax.psum(stacked, "col")
    slice_rows = TILE // lax.axis_size("col")
    summed = lax.dynamic_slice_in_dim(whole, lax.axis_index("col") * slice_rows, slice_rows, 2)
    return summed[0] * summed[1]


def solution(mesh):
    placed = (P("row", "col"), P("row", "col"), P("row", "col"), P("row", None))
    return jax.shard_map(
        shards, mesh=mesh, in_specs=placed, out_specs=P("row", "col", None), check_vma=False
    )
```

profile of v0, /device:TPU:1, one launch (start us, length us, event | category | flops | bytes accessed | tf_op | source)
XLA Modules:
  0.0 358.9 jit_solution(2798819045864562003)
XLA Ops:
  6.5 0.0 copy-start
  6.5 20.3 %all-gather = s32[16,24,2]{1,2,0:T(2,128)S(1)} all-gather(s32[1,24,2]{1,2,0:T(2,128)} %bitcast.26), channel_id=1, replica_groups=mesh['row'=16,'col'=8] {'row'}, dimensions={0}, use_global_device_ids=true | all-gather | bytes 3264 | tf_op jit(solution)/shard_map/all_gather | solution.py:15
  26.8 0.1 reshape.79
  27.0 0.1 reduce_max.15
  27.0 0.1 reduce_max.20
  27.2 6.2 %gather_fusion = bf16[16,256,1024]{2,1,0:T(8,128)(2,1)} fusion(bf16[4,256,1024]{2,1,0:T(8,128)(2,1)} %bitcast.24, s32[1024]{0:T(1024)S(1)} %pad_clamp_fusion.1), kind=kCustom, calls=%fused_computation.2 | custom fusion | bytes 16777280 | tf_op jit(solution)/shard_map/jit(_take)/gather | solution.py:20
  33.4 7.4 %broadcast_select_fusion.1 = bf16[16,256,1024]{2,1,0:T(8,128)(2,1)} fusion(bf16[16,256,1024]{2,1,0:T(8,128)(2,1)} %gather_fusion, pred[16]{0:T(512)(128)(4,1)S(1)} %compare_and_fusion.1), kind=kLoop, calls=%fused_computation.13 | loop fusion | flops 4194304 | bytes 16777232 | tf_op jit(solution)/shard_map/jit(_take)/select_n | solution.py:20
  40.9 0.0 copy-start.3
  40.9 4.9 %all-to-all-start = ((bf16[16,256,1024]{2,1,0:T(8,128)(2,1)}), bf16[16,256,1024]{2,1,0:T(8,128)(2,1)}, u32[]{:S(2)}, u32[]{:S(2)}) async-start(bf16[16,256,1024]{2,1,0:T(8,128)(2,1)} %broadcast_select_fusion.1), calls=%async_computation | async-start | bytes 16777216 | tf_op jit(solution)/shard_map/all_to_all | solution.py:21
  45.8 0.0 all-reduce.2.cloned.1.call-start
  45.9 0.0 copy-done.3
  45.9 0.0 copy-done
  45.9 6.0 %gather_fusion.2 = bf16[24,256,1024]{2,1,0:T(8,128)(2,1)} fusion(bf16[4,256,1024]{2,1,0:T(8,128)(2,1)S(1)} %bitcast.22, s32[1024]{0:T(1024)S(1)} %pad_clamp_fusion.2), kind=kCustom, calls=%fused_computation.clone | custom fusion | bytes 25165920 | tf_op jit(solution)/shard_map/jit(_take)/gather | solution.py:29
  51.9 0.0 copy-start.2
  51.9 7.8 %gather_fusion.3 = bf16[24,256,1024]{2,1,0:T(8,128)(2,1)} fusion(bf16[4,256,1024]{2,1,0:T(8,128)(2,1)} %bitcast.23, s32[1024]{0:T(1024)S(1)} %pad_clamp_fusion.2), kind=kCustom, calls=%fused_computation.1.clone | custom fusion | bytes 25165920 | tf_op jit(solution)/shard_map/jit(_take)/gather | solution.py:30
  59.7 83.6 %all-to-all-done = bf16[16,256,1024]{2,1,0:T(8,128)(2,1)} async-done(((bf16[16,256,1024]{2,1,0:T(8,128)(2,1)}), bf16[16,256,1024]{2,1,0:T(8,128)(2,1)}, u32[]{:S(2)}, u32[]{:S(2)}) %all-to-all-start) | async-done | bytes 8388640 | tf_op jit(solution)/shard_map/all_to_all | solution.py:21
  143.4 0.0 copy-done.2
  143.4 8.6 %pad_maximum_fusion.1 = bf16[20,256,1024]{2,1,0:T(8,128)(2,1)} fusion(bf16[16,256,1024]{2,1,0:T(8,128)(2,1)} %all-to-all-done, bf16[4,256,1024]{2,1,0:T(8,128)(2,1)S(1)} %bitcast.25), kind=kLoop, calls=%fused_computation.12 | loop fusion | flops 5242880 | bytes 20971520 | tf_op jit(solution)/shard_map/concatenate | solution.py:22
  152.0 10.1 %gather_fusion.1 = bf16[24,256,1024]{2,1,0:T(8,128)(2,1)} fusion(bf16[20,256,1024]{2,1,0:T(8,128)(2,1)} %pad_maximum_fusion.1, s32[1024]{0:T(1024)S(1)} %pad_clamp_fusion), kind=kCustom, calls=%fused_computation.3 | custom fusion | bytes 25165920 | tf_op jit(solution)/shard_map/jit(_take)/gather | solution.py:31
  162.1 13.1 %fusion.8 = f32[1,24,256,256]{3,2,1,0:T(8,128)} fusion(bf16[24,256,1024]{2,1,0:T(8,128)(2,1)} %gather_fusion.1, pred[24]{0:T(512)(128)(4,1)S(1)} %get-tuple-element.8, bf16[24,256,1024]{2,1,0:T(8,128)(2,1)} %gather_fusion.2, pred[24]{0:T(512)(128)(4,1)S(1)} %get-tuple-element.6), kind=kOutput, calls=%fused_computation.16 | convolution fusion | flops 3233808384 | bytes 31457328 | tf_op jit(solution)/shard_map/tak,tbk->tab/dot_general | solution.py:32
  175.1 13.0 %fusion.11 = f32[1,24,256,256]{3,2,1,0:T(8,128)} fusion(bf16[24,256,1024]{2,1,0:T(8,128)(2,1)} %gather_fusion.1, pred[24]{0:T(512)(128)(4,1)S(1)} %get-tuple-element.8, bf16[24,256,1024]{2,1,0:T(8,128)(2,1)} %gather_fusion.3, pred[24]{0:T(512)(128)(4,1)S(1)} %get-tuple-element.6), kind=kOutput, calls=%fused_computation.17 | convolution fusion | flops 3233808384 | bytes 31457328 | tf_op jit(solution)/shard_map/tak,tbk->tab/dot_general | solution.py:33
  188.2 0.0 copy-start.1
  188.2 10.7 %pad_maximum_fusion = f32[2,24,256,256]{3,2,1,0:T(8,128)} fusion(f32[1,24,256,256]{3,2,1,0:T(8,128)} %fusion.11, f32[1,24,256,256]{3,2,1,0:T(8,128)} %fusion.8), kind=kLoop, calls=%fused_computation.4 | loop fusion | flops 3145728 | bytes 25165824 | tf_op jit(solution)/shard_map/stack | solution.py:34
  198.9 0.0 all-reduce.2.cloned.1.call-update
  198.9 150.7 %all-reduce.2.cloned.1.call-done = f32[2,24,256,256]{3,2,1,0:T(8,128)} async-done(((f32[2,24,256,256]{3,2,1,0:T(8,128)}), f32[2,24,256,256]{3,2,1,0:T(8,128)}) %all-reduce.2.cloned.1.call-update) | async-done | bytes 12582928 | tf_op jit(solution)/shard_map/psum | solution.py:35
  349.6 2.4 fusion.14
  352.0 0.0 copy-done.1
  (9 shorter events, 0.1 us)
Async XLA Ops:
  6.5 39.4 %copy-start = (bf16[1024,1024]{1,0:T(8,128)(2,1)S(1)}, bf16[1024,1024]{1,0:T(8,128)(2,1)}, u32[]{:S(2)}) copy-start(bf16[1024,1024]{1,0:T(8,128)(2,1)} %param.6) | copy-start | bytes 6291460
  40.9 5.0 %copy-start.3 = (s32[24,2]{0,1:T(2,128)S(1)}, s32[24,2]{0,1:T(2,128)}, u32[]{:S(2)}) copy-start(s32[24,2]{0,1:T(2,128)} %param.9) | copy-start | bytes 580
  40.9 102.5 %all-to-all-start = ((bf16[16,256,1024]{2,1,0:T(8,128)(2,1)}), bf16[16,256,1024]{2,1,0:T(8,128)(2,1)}, u32[]{:S(2)}, u32[]{:S(2)}) async-start(bf16[16,256,1024]{2,1,0:T(8,128)(2,1)} %broadcast_select_fusion.1), calls=%async_computation | async-start | bytes 16777216 | tf_op jit(solution)/shard_map/all_to_all | solution.py:21
  45.8 303.8 %all-reduce.2.cloned.1.call-start = ((), (), s32[]{:S(2)}) async-start(), calls=%async_computation.1 | async-start | bytes 25165824 | tf_op jit(solution)/shard_map/psum | solution.py:35
  51.9 91.5 %copy-start.2 = (bf16[1024,1024]{1,0:T(8,128)(2,1)S(1)}, bf16[1024,1024]{1,0:T(8,128)(2,1)}, u32[]{:S(2)}) copy-start(bf16[1024,1024]{1,0:T(8,128)(2,1)} %param.8) | copy-start | bytes 6291460
  188.2 163.8 %copy-start.1 = (bf16[1024,1024]{1,0:T(8,128)(2,1)S(1)}, bf16[1024,1024]{1,0:T(8,128)(2,1)}, u32[]{:S(2)}) copy-start(bf16[1024,1024]{1,0:T(8,128)(2,1)} %param.6) | copy-start | bytes 6291460
Sparse Core Ops, SparseCore 0:
  199.1 150.5 all-reduce.1
where the time goes:
time: 359 us
  waiting for transfers between devices  234 us (65%)
  local copies, waits for them, and re-layouts  30.3 us (8%)
  other arithmetic  29.4 us (8%)
  matrix products  26.1 us (7%)
  blocking collectives  20.3 us (6%)
  between operations  13.5 us (4%)
  starting transfers between devices  4.98 us (1%)
    psum x1, waiting for transfers between devices, shards(): whole = lax.psum(stacked, 'col')  151 us
    all_to_all x1, waiting for transfers between devices, shards(): lax.all_to_all(outgoing, 'row', split_axis=0, concat_axis=0, tiled=True)  83.6 us
    all_gather x1, blocking collectives, shards(): every_pair = lax.all_gather(pairs, 'row', axis=0, tiled=True)  20.3 us
    dot_general x1, matrix products, shards(): jnp.einsum('tak,tbk->tab', left_x, right_rows, preferred_element_type=jnp...  13.1 us
    dot_general x1, matrix products, shards(): jnp.einsum('tak,tbk->tab', left_s, right_rows, preferred_element_type=jnp...  13 us
    another operation x1, other arithmetic, shards(): stacked = jnp.stack([cross_x, cross_s])  10.7 us
    gather x1, local copies, waits for them, and re-layouts, shards(): right_rows = jnp.take(block_table, second_slot, axis=0)  10.1 us
    concatenate x1, other arithmetic, shards(): block_table = jnp.concatenate([weight_blocks, incoming], axis=0)  8.62 us
  transfers between devices with their start and end apart: 2, of which 2 were waited for; matrix products, arithmetic and copies ran while one was open for 4% of the time, Pallas kernels for 0%

commit v1 on v0

--- a/solution.py
+++ b/solution.py
@@ -32,7 +32,9 @@
     cross_x = jnp.einsum("tak,tbk->tab", left_x, right_rows, preferred_element_type=jnp.float32)
     cross_s = jnp.einsum("tak,tbk->tab", left_s, right_rows, preferred_element_type=jnp.float32)
     stacked = jnp.stack([cross_x, cross_s])
-    whole = lax.psum(stacked, "col")
+    whole = stacked
+    for hop in (1, 2, 4):
+        whole = whole + lax.ppermute(whole, "col", [(dev, dev ^ hop) for dev in range(8)])
     slice_rows = TILE // lax.axis_size("col")
     summed = lax.dynamic_slice_in_dim(whole, lax.axis_index("col") * slice_rows, slice_rows, 2)
     return summed[0] * summed[1]

time: 359 us -> 797 us (2.22)
  waiting for transfers between devices: 234 us -> 643 us
  other arithmetic: 29.4 us -> 58.5 us
  between operations: 13.5 us -> 0.13 us
  starting transfers between devices: 4.98 us -> 17.4 us
    ppermute x0 -> x3, waiting for transfers between devices: none -> 559 us  [shards(): lax.ppermute(whole, 'col', [(dev, dev ^ hop) for dev in range(8)])]
    psum x1 -> x0, waiting for transfers between devices: 151 us -> none  [shards(): whole = lax.psum(stacked, 'col')]
    add x0 -> x3, other arithmetic: none -> 30.6 us  [shards(): whole + lax.ppermute(whole, 'col', [(dev, dev ^ hop) for dev in range(8)])]
    ppermute x0 -> x3, starting transfers between devices: none -> 12.5 us  [shards(): lax.ppermute(whole, 'col', [(dev, dev ^ hop) for dev in range(8)])]
  transfers between devices with their start and end apart: 2 -> 4, of which waited for: 2 -> 4; matrix products, arithmetic and copies ran while one was open for 4% -> 2% of each run, Pallas kernels for 0% -> 0%
where the time goes in v1:
time: 797 us; the launch traced here: 796 us
  waiting for transfers between devices  643 us (81%)
  other arithmetic  58.5 us (7%)
  local copies, waits for them, and re-layouts  30.3 us (4%)
  matrix products  26.1 us (3%)
  blocking collectives  20.3 us (3%)
  starting transfers between devices  17.4 us (2%)
    ppermute x3, waiting for transfers between devices, shards(): lax.ppermute(whole, 'col', [(dev, dev ^ hop) for dev in range(8)])  559 us
    all_to_all x1, waiting for transfers between devices, shards(): lax.all_to_all(outgoing, 'row', split_axis=0, concat_axis=0, tiled=True)  83.7 us
    add x3, other arithmetic, shards(): whole + lax.ppermute(whole, 'col', [(dev, dev ^ hop) for dev in range(8)])  30.6 us
    all_gather x1, blocking collectives, shards(): every_pair = lax.all_gather(pairs, 'row', axis=0, tiled=True)  20.3 us
  transfers between devices with their start and end apart: 4, of which 4 were waited for; matrix products, arithmetic and copies ran while one was open for 2% of the time, Pallas kernels for 0%

profile of v1, /device:TPU:1, one launch (start us, length us, event | category | flops | bytes accessed | tf_op | source)
XLA Modules:
  0.0 795.6 jit_solution(12211022205247524841)
XLA Ops:
  0.0 0.0 copy-start
  0.0 20.3 %all-gather = s32[16,24,2]{1,2,0:T(2,128)S(1)} all-gather(s32[1,24,2]{1,2,0:T(2,128)} %bitcast.28), channel_id=1, replica_groups=mesh['row'=16,'col'=8] {'row'}, dimensions={0}, use_global_device_ids=true | all-gather | bytes 3264 | tf_op jit(solution)/shard_map/all_gather | solution.py:15
  20.3 0.1 reshape.79
  20.4 0.1 reduce_max.15
  20.5 0.1 reduce_max.20
  20.7 6.2 gather_fusion
  26.9 7.4 broadcast_select_fusion.1
  34.3 0.0 copy-start.4
  34.3 4.9 all-to-all-start
  39.3 0.0 copy-done.4
  39.3 0.0 copy-done
  39.3 6.0 gather_fusion.3
  45.3 0.0 copy-start.3
  45.3 7.8 gather_fusion.2
  53.1 83.7 %all-to-all-done = bf16[16,256,1024]{2,1,0:T(8,128)(2,1)} async-done(((bf16[16,256,1024]{2,1,0:T(8,128)(2,1)}), bf16[16,256,1024]{2,1,0:T(8,128)(2,1)}, u32[]{:S(2)}, u32[]{:S(2)}) %all-to-all-start) | async-done | bytes 8388640 | tf_op jit(solution)/shard_map/all_to_all | solution.py:21
  136.8 0.0 copy-done.3
  136.8 8.6 %pad_maximum_fusion.1 = bf16[20,256,1024]{2,1,0:T(8,128)(2,1)} fusion(bf16[16,256,1024]{2,1,0:T(8,128)(2,1)} %all-to-all-done, bf16[4,256,1024]{2,1,0:T(8,128)(2,1)S(1)} %bitcast.27), kind=kLoop, calls=%fused_computation.12 | loop fusion | flops 5242880 | bytes 20971520 | tf_op jit(solution)/shard_map/concatenate | solution.py:22
  145.4 10.1 %gather_fusion.1 = bf16[24,256,1024]{2,1,0:T(8,128)(2,1)} fusion(bf16[20,256,1024]{2,1,0:T(8,128)(2,1)} %pad_maximum_fusion.1, s32[1024]{0:T(1024)S(1)} %pad_clamp_fusion), kind=kCustom, calls=%fused_computation.3 | custom fusion | bytes 25165920 | tf_op jit(solution)/shard_map/jit(_take)/gather | solution.py:31
  155.5 13.1 %fusion.11 = f32[1,24,256,256]{3,2,1,0:T(8,128)} fusion(bf16[24,256,1024]{2,1,0:T(8,128)(2,1)} %gather_fusion.1, pred[24]{0:T(512)(128)(4,1)S(1)} %get-tuple-element.8, bf16[24,256,1024]{2,1,0:T(8,128)(2,1)} %gather_fusion.3, pred[24]{0:T(512)(128)(4,1)S(1)} %get-tuple-element.6), kind=kOutput, calls=%fused_computation.17 | convolution fusion | flops 3233808384 | bytes 31457328 | tf_op jit(solution)/shard_map/tak,tbk->tab/dot_general | solution.py:33
  168.6 13.0 %fusion.8 = f32[1,24,256,256]{3,2,1,0:T(8,128)} fusion(bf16[24,256,1024]{2,1,0:T(8,128)(2,1)} %gather_fusion.1, pred[24]{0:T(512)(128)(4,1)S(1)} %get-tuple-element.8, bf16[24,256,1024]{2,1,0:T(8,128)(2,1)} %gather_fusion.2, pred[24]{0:T(512)(128)(4,1)S(1)} %get-tuple-element.6), kind=kOutput, calls=%fused_computation.16 | convolution fusion | flops 3233808384 | bytes 31457328 | tf_op jit(solution)/shard_map/tak,tbk->tab/dot_general | solution.py:32
  181.6 0.0 slice-start
  181.6 10.6 %pad_maximum_fusion = f32[2,24,256,256]{3,2,1,0:T(8,128)} fusion(f32[1,24,256,256]{3,2,1,0:T(8,128)} %fusion.11, f32[1,24,256,256]{3,2,1,0:T(8,128)} %fusion.8), kind=kLoop, calls=%fused_computation.4 | loop fusion | flops 3145728 | bytes 25165824 | tf_op jit(solution)/shard_map/stack | solution.py:34
  192.2 0.0 slice-start.1
  192.2 0.0 copy-start.2
  192.2 8.3 %collective-permute-start = (f32[2,24,256,256]{3,2,1,0:T(8,128)}, f32[2,24,256,256]{3,2,1,0:T(8,128)}, u32[]{:S(2)}, u32[]{:S(2)}) collective-permute-start(f32[2,24,256,256]{3,2,1,0:T(8,128)} %pad_maximum_fusion), channel_id=1, source_target_pairs={{0,1},{1,0},{2,3},{3,2},{4,5},{5,4},{6,7},{7,6},{8,9},{9,8},{10,11... | collective-permute-start | bytes 37748744 | tf_op jit(solution)/shard_map/ppermute | solution.py:37
  200.6 19.1 %collective-permute-done = f32[2,24,256,256]{3,2,1,0:T(8,128)} collective-permute-done((f32[2,24,256,256]{3,2,1,0:T(8,128)}, f32[2,24,256,256]{3,2,1,0:T(8,128)}, u32[]{:S(2)}, u32[]{:S(2)}) %collective-permute-start) | collective-permute-done | bytes 12582944 | tf_op jit(solution)/shard_map/ppermute | solution.py:37
  219.7 14.1 %fusion.19 = f32[2,24,256,256]{3,2,1,0:T(8,128)} fusion(f32[2,24,256,256]{3,2,1,0:T(8,128)} %collective-permute-done, f32[1,24,256,256]{3,2,1,0:T(8,128)} %fusion.11, f32[1,24,256,256]{3,2,1,0:T(8,128)} %fusion.8), kind=kLoop, calls=%fused_computation.45 | loop fusion | flops 6291456 | bytes 37748736 | tf_op jit(solution)/shard_map/add | solution.py:37
  233.7 1.3 collective-permute-start.1
  235.0 270.5 %collective-permute-done.1 = f32[2,24,256,256]{3,2,1,0:T(8,128)} collective-permute-done((f32[2,24,256,256]{3,2,1,0:T(8,128)}, f32[2,24,256,256]{3,2,1,0:T(8,128)}, u32[]{:S(2)}, u32[]{:S(2)}) %collective-permute-start.1) | collective-permute-done | bytes 12582944 | tf_op jit(solution)/shard_map/ppermute | solution.py:37
  505.6 0.0 slice-done
  505.6 0.0 slice-done.1
  505.6 0.0 copy-done.2
  505.6 0.0 copy-start.1
  505.6 14.4 %fusion.20 = f32[2,24,256,256]{3,2,1,0:T(8,128)} fusion(f32[2,24,256,256]{3,2,1,0:T(8,128)} %collective-permute-done.1, f32[2,24,256,256]{3,2,1,0:T(8,128)} %collective-permute-done, f32[1,24,256,256]{3,2,1,0:T(8,128)S(1)} %bitcast.25, f32[1,24,256,256]{3,2,1,0:T(8,128)S(1)} %copy-done.2), kind=kLoop, calls=%fused_computation.46 | loop fusion | flops 9437184 | bytes 50331648 | tf_op jit(solution)/shard_map/add | solution.py:37
  520.0 2.9 collective-permute-start.2
  522.9 269.6 %collective-permute-done.2 = f32[2,24,256,256]{3,2,1,0:T(8,128)} collective-permute-done((f32[2,24,256,256]{3,2,1,0:T(8,128)}, f32[2,24,256,256]{3,2,1,0:T(8,128)}, u32[]{:S(2)}, u32[]{:S(2)}) %collective-permute-start.2) | collective-permute-done | bytes 12582944 | tf_op jit(solution)/shard_map/ppermute | solution.py:37
  792.5 2.2 dynamic-slice_add_fusion
  794.6 1.0 fusion.14
  795.6 0.0 copy-done.1
  (10 shorter events, 0.1 us)
Async XLA Ops:
  0.0 39.3 %copy-start = (bf16[1024,1024]{1,0:T(8,128)(2,1)S(1)}, bf16[1024,1024]{1,0:T(8,128)(2,1)}, u32[]{:S(2)}) copy-start(bf16[1024,1024]{1,0:T(8,128)(2,1)} %param.7) | copy-start | bytes 6291460
  34.3 4.9 copy-start.4
  34.3 102.4 %all-to-all-start = ((bf16[16,256,1024]{2,1,0:T(8,128)(2,1)}), bf16[16,256,1024]{2,1,0:T(8,128)(2,1)}, u32[]{:S(2)}, u32[]{:S(2)}) async-start(bf16[16,256,1024]{2,1,0:T(8,128)(2,1)} %broadcast_select_fusion.1), calls=%async_computation | async-start | bytes 16777216 | tf_op jit(solution)/shard_map/all_to_all | solution.py:21
  45.3 91.5 %copy-start.3 = (bf16[1024,1024]{1,0:T(8,128)(2,1)S(1)}, bf16[1024,1024]{1,0:T(8,128)(2,1)}, u32[]{:S(2)}) copy-start(bf16[1024,1024]{1,0:T(8,128)(2,1)} %param.8) | copy-start | bytes 6291460
  181.6 324.0 %slice-start = ((s8[6291456]{0:T(1024)(128)(4,1)}), s8[2097152]{0:T(1024)(128)(4,1)S(1)}, s32[]{:S(2)}) async-start(s8[6291456]{0:T(1024)(128)(4,1)} %bitcast.24), calls=%async_computation.1 | async-start | bytes 4194304
  192.2 313.3 %slice-start.1 = ((s8[6291456]{0:T(1024)(128)(4,1)}), s8[4194304]{0:T(1024)(128)(4,1)S(1)}, s32[]{:S(2)}) async-start(s8[6291456]{0:T(1024)(128)(4,1)} %bitcast.24), calls=%async_computation.2 | async-start | bytes 8388608
  192.2 313.3 %copy-start.2 = (f32[1,24,256,256]{3,2,1,0:T(8,128)S(1)}, f32[1,24,256,256]{3,2,1,0:T(8,128)}, u32[]{:S(2)}) copy-start(f32[1,24,256,256]{3,2,1,0:T(8,128)} %fusion.8) | copy-start | bytes 18874372
  192.2 27.4 %collective-permute-start = (f32[2,24,256,256]{3,2,1,0:T(8,128)}, f32[2,24,256,256]{3,2,1,0:T(8,128)}, u32[]{:S(2)}, u32[]{:S(2)}) collective-permute-start(f32[2,24,256,256]{3,2,1,0:T(8,128)} %pad_maximum_fusion), channel_id=1, source_target_pairs={{0,1},{1,0},{2,3},{3,2},{4,5},{5,4},{6,7},{7,6},{8,9},{9,8},{10,11... | collective-permute-start | bytes 37748744 | tf_op jit(solution)/shard_map/ppermute | solution.py:37
  233.7 271.8 %collective-permute-start.1 = (f32[2,24,256,256]{3,2,1,0:T(8,128)}, f32[2,24,256,256]{3,2,1,0:T(8,128)}, u32[]{:S(2)}, u32[]{:S(2)}) collective-permute-start(f32[2,24,256,256]{3,2,1,0:T(8,128)} %fusion.19), channel_id=1, source_target_pairs={{0,2},{1,3},{2,0},{3,1},{4,6},{5,7},{6,4},{7,5},{8,10},{9,11},{10,... | collective-permute-start | bytes 37748744 | tf_op jit(solution)/shard_map/ppermute | solution.py:37
  505.6 290.0 %copy-start.1 = (bf16[1024,1024]{1,0:T(8,128)(2,1)S(1)}, bf16[1024,1024]{1,0:T(8,128)(2,1)}, u32[]{:S(2)}) copy-start(bf16[1024,1024]{1,0:T(8,128)(2,1)} %param.7) | copy-start | bytes 6291460
  520.0 272.5 %collective-permute-start.2 = (f32[2,24,256,256]{3,2,1,0:T(8,128)}, f32[2,24,256,256]{3,2,1,0:T(8,128)}, u32[]{:S(2)}, u32[]{:S(2)}) collective-permute-start(f32[2,24,256,256]{3,2,1,0:T(8,128)} %fusion.20), channel_id=1, source_target_pairs={{0,4},{1,5},{2,6},{3,7},{4,0},{5,1},{6,2},{7,3},{8,12},{9,13},{10,... | collective-permute-start | bytes 37748744 | tf_op jit(solution)/shard_map/ppermute | solution.py:37
